TPU v7x, 256 devices: a whole 4x4x8 slice. The times are simulated.
256 devices in a mesh: tests: 64 (over z, x, core), branches: 4 (over y).
Axes of the slice: x: 4, y: 4, z: 8, core: 2. Of those that a mesh axis runs over, the one named last changes fastest.
Arguments:
- select: float32 [1048576], P('tests'), may hold values from 1e-05 to 0.95
- tiles: float32 [16384, 128, 128], P(('tests', 'branches')), may hold values from 0.0001 to 0.9
- row_block: int32 [16384], P(('tests', 'branches')), may hold values from 0 to 127
- col_block: int32 [16384], P(('tests', 'branches')), may hold values from 0 to 2047, as said below
- counts: int32 [256], P(('tests', 'branches')), may hold values from 1 to 64, 10240 in all
- weights: float32 [1048576], P('branches'), may hold values from 1 to 16
Outputs:
- grad_tests: float32 [1048576], P('tests')
- tile_grads: float32 [16384, 128, 128], P(('tests', 'branches'))
- next_select: float32 [1048576], P('tests')
Inputs may be any that keep to these rules, and one draw needn't show every extreme that they name: counts[d] is the number of device d's slots, from its first, that hold tiles. Call col_block[s] // 32 the share of slot s. Of the 64 slots of one device at most 2 have one share; in every index of branches one share holds exactly 2 slots of every device there.
All inputs are finite; a program needn't handle non-finite values.
Results may differ from a plain program's by a relative error of at most 0.0003.
Values sent between devices are 32-bit elements; how exact they have to be, the bound alone decides.
A program may use at most 64 MiB of HBM per device.

v0:
```python
import jax
import jax.numpy as jnp
from jax import lax
from jax.sharding import PartitionSpec as P

STEPS = 2
ascent_rate = 0.0015
select_cap = 0.5


def tile_logs(blocks, tiles, rows, live):
    picked = blocks[rows]
    logs = jnp.sum(jnp.log1p(-picked[:, :, None] * tiles), axis=1)
    return jnp.where(live[:, None], logs, jnp.zeros_like(logs))


def tile_terms(blocks, slot_survive, tiles, rows, live):
    picked = blocks[rows]
    inverse = 1.0 / (1.0 - picked[:, :, None] * tiles)
    scaled = slot_survive[:, None, :] * inverse
    tests_part = jnp.sum(scaled * tiles, axis=2)
    tests_part = jnp.where(live[:, None], tests_part, jnp.zeros_like(tests_part))
    tile_part = scaled * picked[:, :, None]
    tile_part = jnp.where(live[:, None, None], tile_part, jnp.zeros_like(tile_part))
    return (tests_part, tile_part)


def body(select, tiles, row_block, col_block, counts, weights):
    width = tiles.shape[1]
    slots = tiles.shape[0]
    test_rows = select.shape[0] // width
    branch_rows = weights.shape[0] // width
    weight_rows = weights.reshape(branch_rows, width)
    limit = counts[0]
    current = select
    grad_tests = select
    tile_grads = tiles
    for step in range(STEPS):
        keep = step == STEPS - 1
        blocks = current.reshape(test_rows, width)
        live = jnp.arange(slots, dtype=jnp.int32) < limit
        slot_logs = tile_logs(blocks, tiles, row_block, live)
        partial_value = jnp.zeros((branch_rows, width), jnp.float32).at[col_block].add(slot_logs)
        summed = lax.psum(partial_value, "tests")
        slot_survive = (weight_rows * jnp.exp(summed))[col_block]
        empty_tests = jnp.zeros((test_rows, width), jnp.float32)
        live = jnp.arange(slots, dtype=jnp.int32) < limit
        tests_part, tile_part = tile_terms(blocks, slot_survive, tiles, row_block, live)
        tests_sum = empty_tests.at[row_block].add(tests_part)
        gradient = lax.psum(tests_sum, "branches").reshape(-1)
        if keep:
            grad_tests = gradient
            tile_grads = tile_part
        rate = ascent_rate * gradient
        current = current + (select_cap - current) * rate / (1.0 + rate)
    return (grad_tests, tile_grads, current)


def solution(mesh):
    return jax.shard_map(
        body,
        mesh=mesh,
        in_specs=(
            P("tests"),
            P(("tests", "branches"), None, None),
            P(("tests", "branches")),
            P(("tests", "branches")),
            P(("tests", "branches")),
            P("branches"),
        ),
        out_specs=(P("tests"), P(("tests", "branches"), None, None), P("tests")),
        check_vma=False,
    )
```

profile of v0, /device:TPU:2, one launch (start us, length us, event | category | flops | bytes accessed | tf_op | source)
XLA Modules:
  0.0 514.2 jit_solution(9038397558886190916)
XLA Ops:
  7.2 0.0 copy-start
  7.2 0.0 all-reduce.5.cloned.1.call-start
  8.0 0.7 compare_select_fusion.1
  8.6 0.7 compare_select_fusion
  9.3 1.4 gather_fusion
  10.7 3.3 log-plus-one_reduce_fusion.1
  14.1 1.9 scatter_custom_fusion
  15.9 0.0 all-reduce.5.cloned.1.call-update
  16.0 0.0 copy-start.1
  16.0 0.0 all-reduce.7.cloned.1.call-start
  16.0 189.7 %all-reduce.5.cloned.1.call-done = f32[2048,128]{1,0:T(8,128)} async-done(((f32[2048,128]{1,0:T(8,128)}), f32[2048,128]{1,0:T(8,128)}) %all-reduce.5.cloned.1.call-update) | async-done | bytes 1048592 | tf_op jit(solution)/shard_map/psum | solution.py:44
  205.7 0.0 copy-done
  205.7 1.4 bitcast_multiply_fusion.1
  207.1 0.6 gather_fusion.1
  207.7 4.5 multiply_reduce_fusion.1
  212.2 1.5 scatter_custom_fusion.1
  213.7 0.0 all-reduce.7.cloned.1.call-update
  213.7 0.0 all-reduce.9.cloned.1.call-start
  213.8 43.7 %all-reduce.7.cloned.1.call-done = f32[128,128]{1,0:T(8,128)} async-done(((f32[128,128]{1,0:T(8,128)}), f32[128,128]{1,0:T(8,128)}) %all-reduce.7.cloned.1.call-update) | async-done | bytes 65552 | tf_op jit(solution)/shard_map/psum | solution.py:50
  257.4 0.0 copy-done.1
  257.4 0.9 fusion.22
  258.3 0.6 gather_fusion.2
  258.9 3.3 log-plus-one_reduce_fusion
  262.2 1.9 scatter_custom_fusion.2
  264.1 0.0 all-reduce.9.cloned.1.call-update
  264.1 0.0 all-reduce.11.cloned.1.call-start
  264.2 187.4 %all-reduce.9.cloned.1.call-done = f32[2048,128]{1,0:T(8,128)} async-done(((f32[2048,128]{1,0:T(8,128)}), f32[2048,128]{1,0:T(8,128)}) %all-reduce.9.cloned.1.call-update) | async-done | bytes 1048592 | tf_op jit(solution)/shard_map/psum | solution.py:44
  451.6 1.4 bitcast_multiply_fusion
  453.0 0.6 gather_fusion.3
  453.6 0.0 copy-start.2
  453.6 5.9 %multiply_select_fusion = (f32[64,128,128]{2,1,0:T(8,128)}, f32[64,128]{1,0:T(8,128)S(1)}) fusion(f32[64,128,128]{2,1,0:T(8,128)} %param.7, f32[64,128]{1,0:T(8,128)S(1)} %gather_fusion.2, f32[64,128]{1,0:T(8,128)S(1)} %gather_fusion.3, pred[64]{0:T(512)(128)(4,1)S(1)} %iota_compare_fusion), kind=kLoop, calls=%fused_computation.8 | loop fusion | flops 8380416 | bytes 8486976 | tf_op jit(solution)/shard_map/jit(_where)/select_n | solution.py:24
  459.5 1.5 scatter_custom_fusion.3
  460.9 0.0 all-reduce.11.cloned.1.call-update
  460.9 43.7 %all-reduce.11.cloned.1.call-done = f32[16384]{0:T(1024)} async-done(((f32[16384]{0:T(1024)}), f32[16384]{0:T(1024)}) %all-reduce.11.cloned.1.call-update) | async-done | bytes 65552 | tf_op jit(solution)/shard_map/psum | solution.py:50
  504.7 0.0 copy-done.2
  504.7 1.5 divide_add_fusion
  506.2 1.5 copy.14
  (5 shorter events, 0.0 us)
Async XLA Ops:
  7.2 198.6 %copy-start = (f32[262144]{0:T(1024)S(1)}, f32[262144]{0:T(1024)}, u32[]{:S(2)}) copy-start(f32[262144]{0:T(1024)} %param.11) | copy-start | bytes 3145732
  7.2 198.6 %all-reduce.5.cloned.1.call-start = ((), (), s32[]{:S(2)}) async-start(), calls=%async_computation | async-start | bytes 2097152 | tf_op jit(solution)/shard_map/psum | solution.py:44
  16.0 241.5 %copy-start.1 = (f32[16384]{0:T(1024)S(1)}, f32[16384]{0:T(1024)}, u32[]{:S(2)}) copy-start(f32[16384]{0:T(1024)} %param.6) | copy-start | bytes 196612
  16.0 241.4 %all-reduce.7.cloned.1.call-start = ((), (), s32[]{:S(2)}) async-start(), calls=%async_computation.1 | async-start | bytes 131072 | tf_op jit(solution)/shard_map/psum | solution.py:50
  213.7 237.9 %all-reduce.9.cloned.1.call-start = ((), (), s32[]{:S(2)}) async-start(), calls=%async_computation.2 | async-start | bytes 2097152 | tf_op jit(solution)/shard_map/psum | solution.py:44
  264.1 240.5 %all-reduce.11.cloned.1.call-start = ((), (), s32[]{:S(2)}) async-start(), calls=%async_computation.3 | async-start | bytes 131072 | tf_op jit(solution)/shard_map/psum | solution.py:50
  453.6 51.1 %copy-start.2 = (f32[128,128]{1,0:T(8,128)S(1)}, f32[128,128]{1,0:T(8,128)}, u32[]{:S(2)}) copy-start(f32[128,128]{1,0:T(8,128)} %all-reduce.7.cloned.1.call-done) | copy-start | bytes 196612
Sparse Core Ops, SparseCore 0:
  16.1 189.6 all-reduce.4
  213.8 43.5 all-reduce.6
  264.3 187.3 all-reduce.8
  461.1 43.5 all-reduce.10
where the time goes:
time: 515 us; the launch traced here: 514 us
  waiting for transfers between devices  465 us (90%)
  other arithmetic  30.2 us (6%)
  between operations  14.6 us (3%)
    psum x2, waiting for transfers between devices, body(): summed = lax.psum(partial_value, 'tests')  377 us
    psum x2, waiting for transfers between devices, body(): gradient = lax.psum(tests_sum, 'branches').reshape(-1)  87.4 us
  transfers between devices with their start and end apart: 4, of which 4 were waited for; matrix products, arithmetic and copies ran while one was open for 0% of the time, Pallas kernels for 0%

commit v1 on v0

--- a/solution.py
+++ b/solution.py
@@ -47,7 +47,7 @@
         live = jnp.arange(slots, dtype=jnp.int32) < limit
         tests_part, tile_part = tile_terms(blocks, slot_survive, tiles, row_block, live)
         tests_sum = empty_tests.at[row_block].add(tests_part)
-        gradient = lax.psum(tests_sum, "branches").reshape(-1)
+        gradient = jnp.sum(lax.all_gather(tests_sum, "branches"), axis=0).reshape(-1)
         if keep:
             grad_tests = gradient
             tile_grads = tile_part

time: 515 us -> 445 us (0.86)
  waiting for transfers between devices: 465 us -> 373 us
  blocking collectives: 0 us -> 25.7 us
    psum x2 -> x0, waiting for transfers between devices: 87.4 us -> none  [body(): gradient = lax.psum(tests_sum, 'branches').reshape(-1)]
    all_gather x0 -> x2, blocking collectives: none -> 25.7 us  [body(): lax.all_gather(tests_sum, 'branches')]
  transfers between devices with their start and end apart: 4 -> 2, of which waited for: 4 -> 2; matrix products, arithmetic and copies ran while one was open for 0% -> 0% of each run, Pallas kernels for 0% -> 0%
where the time goes in v1:
time: 445 us; the launch traced here: 444 us
  waiting for transfers between devices  373 us (84%)
  other arithmetic  27.3 us (6%)
  blocking collectives  25.7 us (6%)
  between operations  14.9 us (3%)
    psum x2, waiting for transfers between devices, body(): summed = lax.psum(partial_value, 'tests')  373 us
    all_gather x2, blocking collectives, body(): lax.all_gather(tests_sum, 'branches')  25.7 us
  transfers between devices with their start and end apart: 2, of which 2 were waited for; matrix products, arithmetic and copies ran while one was open for 0% of the time, Pallas kernels for 0%

profile of v1, /device:TPU:2, one launch (start us, length us, event | category | flops | bytes accessed | tf_op | source)
XLA Modules:
  0.0 444.4 jit_solution(1126891048918274531)
XLA Ops:
  7.2 0.0 copy-start
  7.2 0.0 all-reduce.3.cloned.1.call-start
  8.0 0.7 compare_select_fusion.1
  8.6 0.7 compare_select_fusion
  9.3 1.4 gather_fusion
  10.7 3.3 log-plus-one_reduce_fusion.1
  14.1 1.9 scatter_custom_fusion
  15.9 0.0 all-reduce.3.cloned.1.call-update
  16.0 0.0 all-reduce.5.cloned.1.call-start
  16.0 0.0 copy-start.1
  16.0 189.7 %all-reduce.3.cloned.1.call-done = f32[2048,128]{1,0:T(8,128)} async-done(((f32[2048,128]{1,0:T(8,128)}), f32[2048,128]{1,0:T(8,128)}) %all-reduce.3.cloned.1.call-update) | async-done | bytes 1048592 | tf_op jit(solution)/shard_map/psum | solution.py:44
  205.7 0.0 copy-done
  205.7 1.4 bitcast_multiply_fusion.1
  207.1 0.6 gather_fusion.1
  207.7 4.5 %multiply_reduce_fusion.1 = f32[64,128]{1,0:T(8,128)S(1)} fusion(f32[64,128,128]{2,1,0:T(8,128)} %param.7, f32[64,128]{1,0:T(8,128)S(1)} %gather_fusion, f32[64,128]{1,0:T(8,128)S(1)} %gather_fusion.1), kind=kLoop, calls=%fused_computation.12 | loop fusion | flops 6283264 | bytes 4292608 | tf_op jit(solution)/shard_map/reduce_sum | solution.py:21
  212.2 0.9 scatter_custom_fusion.1
  213.1 12.9 %all-gather = f32[512,128]{1,0:T(8,128)S(1)} all-gather(f32[128,128]{1,0:T(8,128)S(1)} %scatter_custom_fusion.1), channel_id=2, replica_groups=mesh['tests'=64,'branches'=4] {'branches'}, dimensions={0}, use_global_device_ids=true | all-gather | bytes 327680 | tf_op jit(solution)/shard_map/all_gather | solution.py:50
  226.0 0.0 copy-done.1
  226.1 0.6 gather_fusion.2
  226.7 3.3 log-plus-one_reduce_fusion
  230.0 1.9 scatter_custom_fusion.2
  231.9 0.0 all-reduce.5.cloned.1.call-update
  231.9 183.4 %all-reduce.5.cloned.1.call-done = f32[2048,128]{1,0:T(8,128)} async-done(((f32[2048,128]{1,0:T(8,128)}), f32[2048,128]{1,0:T(8,128)}) %all-reduce.5.cloned.1.call-update) | async-done | bytes 1048592 | tf_op jit(solution)/shard_map/psum | solution.py:44
  415.3 1.4 bitcast_multiply_fusion
  416.6 0.6 gather_fusion.3
  417.2 5.8 %multiply_select_fusion = (f32[64,128,128]{2,1,0:T(8,128)}, f32[64,128]{1,0:T(8,128)S(1)}) fusion(f32[64,128,128]{2,1,0:T(8,128)} %param.7, f32[64,128]{1,0:T(8,128)S(1)} %gather_fusion.2, f32[64,128]{1,0:T(8,128)S(1)} %gather_fusion.3, pred[64]{0:T(512)(128)(4,1)S(1)} %iota_compare_fusion), kind=kLoop, calls=%fused_computation.8 | loop fusion | flops 8380416 | bytes 8486976 | tf_op jit(solution)/shard_map/jit(_where)/select_n | solution.py:24
  423.1 0.9 scatter_custom_fusion.3
  424.0 12.9 %all-gather.1 = f32[512,128]{1,0:T(8,128)S(1)} all-gather(f32[128,128]{1,0:T(8,128)S(1)} %scatter_custom_fusion.3), channel_id=3, replica_groups=mesh['tests'=64,'branches'=4] {'branches'}, dimensions={0}, use_global_device_ids=true | all-gather | bytes 327680 | tf_op jit(solution)/shard_map/all_gather | solution.py:50
  436.9 0.0 copy-start.2
  436.9 0.7 divide_add_fusion
  437.6 0.0 copy-done.2
  (8 shorter events, 0.1 us)
Async XLA Ops:
  7.2 198.6 %copy-start = (f32[262144]{0:T(1024)S(1)}, f32[262144]{0:T(1024)}, u32[]{:S(2)}) copy-start(f32[262144]{0:T(1024)} %param.11) | copy-start | bytes 3145732
  7.2 198.6 %all-reduce.3.cloned.1.call-start = ((), (), s32[]{:S(2)}) async-start(), calls=%async_computation | async-start | bytes 2097152 | tf_op jit(solution)/shard_map/psum | solution.py:44
  16.0 399.3 %all-reduce.5.cloned.1.call-start = ((), (), s32[]{:S(2)}) async-start(), calls=%async_computation.1 | async-start | bytes 2097152 | tf_op jit(solution)/shard_map/psum | solution.py:44
  16.0 210.0 %copy-start.1 = (f32[16384]{0:T(1024)S(1)}, f32[16384]{0:T(1024)}, u32[]{:S(2)}) copy-start(f32[16384]{0:T(1024)} %param.6) | copy-start | bytes 196612
  436.9 0.7 copy-start.2
Sparse Core Ops, SparseCore 0:
  16.1 189.6 all-reduce.2
  232.0 183.2 all-reduce.4
